TPU v7x, 32 devices: a whole 2x2x4 slice. The times are simulated.
32 devices in a mesh: shot: 4 (over y, core), recv: 8 (over z, x).
Axes of the slice: x: 2, y: 2, z: 4, core: 2. Of those that a mesh axis runs over, the one named last changes fastest.
Arguments:
- wavefield: bfloat16 [2, 8, 1, 1024, 4096], P(None, 'recv', None, None, 'shot'), may hold values from -1 to 1
- live: int32 [4096], replicated, may hold values 0 or 1
- block_order: int32 [32], replicated, may hold values from 0 to 31, each once
- wavelet: float32 [2, 2], replicated, may hold values from 0.5 to 1.5
Outputs:
- multiples: bfloat16 [2, 8, 1, 1024, 4096], P(None, 'recv', None, None, 'shot')
Inputs may be any that keep to these rules, and one draw needn't show every extreme that they name: `block_order`: each block number appears once.
All inputs are finite; a program needn't handle non-finite values.
Results may differ from a plain program's by a relative error of at most 0.001.
Values may be sent and summed in bfloat16 or wider, within the bound.
No kernel may reach another device: no remote copies, remote signals or barrier semaphores. Data moves between devices by JAX's collectives and lax.ppermute only.
A program may use at most 64 MiB of HBM per device.

v0:
```python
import jax
import jax.numpy as jnp
from jax import lax
from jax.sharding import PartitionSpec as P

BLOCK = 128
RGROUPS = 4
ROUNDS = 2
BPR = 2


def spread(block, axis, holder):
    block = jnp.where(lax.axis_index(axis) == holder, block, jnp.zeros_like(block))
    return lax.psum(block, axis)


def partner(block, axis, apart):
    count = lax.axis_size(axis)
    route = []
    for low in range(count):
        high = low | 1 << apart
        if high != low and high < count:
            route += [(low, high), (high, low)]
    return lax.ppermute(block, axis, route)


def accumulate(total, columns, rows):

    def product(first, second):
        return jnp.einsum("frk,fks->frs", first, second, preferred_element_type=jnp.float32)

    real = product(columns[0], rows[0]) - product(columns[1], rows[1])
    imag = product(columns[0], rows[1]) + product(columns[1], rows[0])
    return total + jnp.stack([real, imag])


def shards(wavefield, live, block_order, wavelet):
    tile = wavefield[:, 0]
    freq_dev = tile.shape[1]
    recv_rows = tile.shape[2]
    shot_cols = tile.shape[3]
    count = ROUNDS * BPR
    bits = RGROUPS.bit_length() - 1
    position = lax.axis_index("recv")
    my_group = position % RGROUPS
    freq_group = position // RGROUPS
    scales = lax.dynamic_slice_in_dim(wavelet, freq_group * freq_dev, freq_dev, 1)

    def own_rows(block):
        start = block * BLOCK
        owner = start // recv_rows
        offset = start % recv_rows
        piece = lax.dynamic_slice_in_dim(tile, offset, BLOCK, 2)
        return jnp.where(owner == my_group, piece, jnp.zeros_like(piece))

    def columns_of(block):
        start = block * BLOCK
        root = start // shot_cols
        offset = start % shot_cols
        mine = lax.dynamic_slice_in_dim(tile, offset, BLOCK, 3)
        columns = spread(mine, "shot", root)
        weight = lax.dynamic_slice_in_dim(live, start, BLOCK, 0).astype(jnp.bfloat16)
        return columns * weight[None, None, None, :]

    def rows_of(block):
        value = own_rows(block)
        for bit in range(bits):
            value = value + partner(value, "recv", bit)
        return value

    def fetch(step):
        block = block_order[step]
        return (columns_of(block), rows_of(block))

    empty = jnp.zeros((2, freq_dev, recv_rows, shot_cols), jnp.float32)

    def turn(step, carry):
        total, columns, rows = carry
        next_columns, next_rows = fetch(step + 1)
        return (accumulate(total, columns, rows), next_columns, next_rows)

    first_columns, first_rows = fetch(0)
    total, columns, rows = lax.fori_loop(0, count - 1, turn, (empty, first_columns, first_rows))
    total = accumulate(total, columns, rows)
    scale_re = scales[0][:, None, None]
    scale_im = scales[1][:, None, None]
    out_re = -(scale_re * total[0] - scale_im * total[1])
    out_im = -(scale_re * total[1] + scale_im * total[0])
    result = jnp.stack([out_re, out_im]).astype(jnp.bfloat16)
    return result[:, None]


def solution(mesh):
    placed = (P(None, "recv", None, None, "shot"), P(), P(), P())
    return jax.shard_map(
        shards,
        mesh=mesh,
        in_specs=placed,
        out_specs=P(None, "recv", None, None, "shot"),
        check_vma=False,
    )
```

profile of v0, /device:TPU:0, one launch (start us, length us, event | category | flops | bytes accessed | tf_op | source)
XLA Modules:
  0.0 183.8 jit_solution(3456191400455826749)
XLA Ops:
  8.5 3.0 %collective-permute-start.2 = (bf16[2,1,128,1024]{3,2,1,0:T(8,128)(2,1)S(1)}, bf16[2,1,128,1024]{3,2,1,0:T(8,128)(2,1)S(1)}, u32[]{:S(2)}, u32[]{:S(2)}) collective-permute-start(bf16[2,1,128,1024]{3,2,1,0:T(8,128)(2,1)S(1)} %select_bitcast_fusion), channel_id=1, source_target_pairs={{0,1},{1,0},{2,3},{3,2},{4,5},{5,4},{6,7},{7,6},{8,9},{9,8},{10,11... | collective-permute-start | bytes 1572872 | tf_op jit(solution)/shard_map/ppermute | solution.py:24
  11.6 2.3 %select_bitcast_fusion.1 = bf16[2,1,1024,128]{3,2,1,0:T(8,128)(2,1)} fusion(bf16[2,1,1,1024,1024]{4,3,0,2,1:T(8,128)(2,1)} %bitcast.89, s32[]{:T(128)S(6)} %select_n.175, pred[]{:T(512)S(6)} %eq.38), kind=kLoop, calls=%fused_computation.34 | loop fusion | flops 262144 | bytes 1048581 | tf_op jit(solution)/shard_map/jit(_where)/select_n | solution.py:13
  13.9 9.6 %collective-permute-done.2 = bf16[2,1,128,1024]{3,2,1,0:T(8,128)(2,1)S(1)} collective-permute-done((bf16[2,1,128,1024]{3,2,1,0:T(8,128)(2,1)S(1)}, bf16[2,1,128,1024]{3,2,1,0:T(8,128)(2,1)S(1)}, u32[]{:S(2)}, u32[]{:S(2)}) %collective-permute-start.2) | collective-permute-done | bytes 524320 | tf_op jit(solution)/shard_map/ppermute | solution.py:24
  24.8 1.9 %collective-permute-start.3 = (bf16[2,1,128,1024]{3,2,1,0:T(8,128)(2,1)S(1)}, bf16[2,1,128,1024]{3,2,1,0:T(8,128)(2,1)S(1)}, u32[]{:S(2)}, u32[]{:S(2)}) collective-permute-start(bf16[2,1,128,1024]{3,2,1,0:T(8,128)(2,1)S(1)} %fusion.40), channel_id=1, source_target_pairs={{0,2},{2,0},{1,3},{3,1},{4,6},{6,4},{5,7},{7,5},{8,10},{10,8},{9,1... | collective-permute-start | bytes 1572872 | tf_op jit(solution)/shard_map/ppermute | solution.py:24
  28.2 19.6 %all-reduce.3.cloned.1.call-done = bf16[2,1,1024,128]{3,2,1,0:T(8,128)(2,1)} async-done(((bf16[2,1,1024,128]{3,2,1,0:T(8,128)(2,1)}), bf16[2,1,1024,128]{3,2,1,0:T(8,128)(2,1)}) %all-reduce.3.cloned.1.call-update) | async-done | bytes 524304 | tf_op jit(solution)/shard_map/psum | solution.py:14
  49.1 115.6 %while.20 = (s32[]{:T(128)}, f32[2,1,1024,1024]{3,2,1,0:T(8,128)}, bf16[2,1,1024,128]{3,2,1,0:T(8,128)(2,1)S(1)}, bf16[2,1,128,1024]{3,2,1,0:T(8,128)(2,1)S(1)},...) while((s32[]{:T(128)}, f32[2,1,1024,1024]{3,2,1,0:T(8,128)}, ...), condition=%wide.region_3.4_spmd.clone, body=%wide.region_1.3_spmd.clone.sunk | while | flops 1084752000 | bytes 82839248 | solution.py:83
  50.4 2.3 %dynamic-slice_select_fusion.4 = bf16[2,1,1024,128]{3,2,1,0:T(8,128)(2,1)} fusion(bf16[2,1,1024,1024]{3,2,1,0:T(8,128)(2,1)} %get-tuple-element.349, s32[]{:T(128)S(6)} %select_n.227, pred[]{:T(512)S(6)} %eq.44), kind=kLoop, calls=%fused_computation.4.clone.1 | loop fusion | flops 262144 | bytes 1048581 | tf_op jit(solution)/shard_map/while/body/eval_jaxpr/jit(_where)/select_n | solution.py:13
  55.5 2.7 %fusion.60 = f32[1024,1024]{1,0:T(8,128)} fusion(bf16[2,1,128,1024]{3,2,1,0:T(8,128)(2,1)S(1)} %get-tuple-element.329, bf16[2,1,1024,128]{3,2,1,0:T(8,128)(2,1)S(1)} %get-tuple-element.328), kind=kOutput, calls=%fused_computation.5.clone.1 | convolution fusion | flops 268435456 | bytes 4718592 | tf_op jit(solution)/shard_map/while/body/eval_jaxpr/frk,fks->frs/dot_general | solution.py:30
  58.2 2.7 %fusion.61 = f32[1024,1024]{1,0:T(8,128)} fusion(bf16[2,1,128,1024]{3,2,1,0:T(8,128)(2,1)S(1)} %get-tuple-element.329, bf16[2,1,1024,128]{3,2,1,0:T(8,128)(2,1)S(1)} %get-tuple-element.328), kind=kOutput, calls=%fused_computation.11.clone.1 | convolution fusion | flops 268435456 | bytes 4718592 | tf_op jit(solution)/shard_map/while/body/eval_jaxpr/frk,fks->frs/dot_general | solution.py:30
  60.9 3.1 %add_bitcast_fusion.3 = f32[1,1,1024,1024]{3,2,1,0:T(8,128)S(1)} fusion(f32[1024,1024]{1,0:T(8,128)} %fusion.60, bf16[2,1,1024,128]{3,2,1,0:T(8,128)(2,1)S(1)} %get-tuple-element.328, bf16[2,1,128,1024]{3,2,1,0:T(8,128)(2,1)S(1)} %get-tuple-element.329), kind=kOutput, calls=%fused_computation.1.clone.1 | convolution fusion | flops 269484032 | bytes 8912896 | tf_op jit(solution)/shard_map/while/body/eval_jaxpr/frk,fks->frs/dot_general | solution.py:30
  67.8 1.8 collective-permute-start.1
  69.6 4.2 %maximum_add_fusion.3 = f32[2,1,1024,1024]{3,2,1,0:T(8,128)} fusion(f32[1,1,1024,1024]{3,2,1,0:T(8,128)S(1)} %add_bitcast_fusion.3, f32[1,1,1024,1024]{3,2,1,0:T(8,128)S(1)} %subtract_bitcast_fusion.3, f32[2,1,1024,1024]{3,2,1,0:T(8,128)} %get-tuple-element.327, pred[]{:T(512)S(6)} %compare.20), kind=kLoop, calls=%fused_computation.clone.1 | loop fusion | flops 6291456 | bytes 25165824 | tf_op jit(solution)/shard_map/while/body/eval_jaxpr/add | solution.py:34
  74.6 11.8 %all-reduce.5.cloned.1.call-done = bf16[2,1,1024,128]{3,2,1,0:T(8,128)(2,1)} async-done(((bf16[2,1,1024,128]{3,2,1,0:T(8,128)(2,1)}), bf16[2,1,1024,128]{3,2,1,0:T(8,128)(2,1)}) %all-reduce.5.cloned.1.call-update) | async-done | bytes 524304 | tf_op jit(solution)/shard_map/while/body/eval_jaxpr/psum | solution.py:14
  89.0 2.3 %dynamic-slice_select_fusion.4 = bf16[2,1,1024,128]{3,2,1,0:T(8,128)(2,1)} fusion(bf16[2,1,1024,1024]{3,2,1,0:T(8,128)(2,1)} %get-tuple-element.349, s32[]{:T(128)S(6)} %select_n.227, pred[]{:T(512)S(6)} %eq.44), kind=kLoop, calls=%fused_computation.4.clone.1 | loop fusion | flops 262144 | bytes 1048581 | tf_op jit(solution)/shard_map/while/body/eval_jaxpr/jit(_where)/select_n | solution.py:13
  92.6 1.5 collective-permute-start
  94.1 2.7 %fusion.60 = f32[1024,1024]{1,0:T(8,128)} fusion(bf16[2,1,128,1024]{3,2,1,0:T(8,128)(2,1)S(1)} %get-tuple-element.329, bf16[2,1,1024,128]{3,2,1,0:T(8,128)(2,1)S(1)} %get-tuple-element.328), kind=kOutput, calls=%fused_computation.5.clone.1 | convolution fusion | flops 268435456 | bytes 4718592 | tf_op jit(solution)/shard_map/while/body/eval_jaxpr/frk,fks->frs/dot_general | solution.py:30
  96.8 2.7 %fusion.61 = f32[1024,1024]{1,0:T(8,128)} fusion(bf16[2,1,128,1024]{3,2,1,0:T(8,128)(2,1)S(1)} %get-tuple-element.329, bf16[2,1,1024,128]{3,2,1,0:T(8,128)(2,1)S(1)} %get-tuple-element.328), kind=kOutput, calls=%fused_computation.11.clone.1 | convolution fusion | flops 268435456 | bytes 4718592 | tf_op jit(solution)/shard_map/while/body/eval_jaxpr/frk,fks->frs/dot_general | solution.py:30
  99.4 3.1 %add_bitcast_fusion.3 = f32[1,1,1024,1024]{3,2,1,0:T(8,128)S(1)} fusion(f32[1024,1024]{1,0:T(8,128)} %fusion.60, bf16[2,1,1024,128]{3,2,1,0:T(8,128)(2,1)S(1)} %get-tuple-element.328, bf16[2,1,128,1024]{3,2,1,0:T(8,128)(2,1)S(1)} %get-tuple-element.329), kind=kOutput, calls=%fused_computation.1.clone.1 | convolution fusion | flops 269484032 | bytes 8912896 | tf_op jit(solution)/shard_map/while/body/eval_jaxpr/frk,fks->frs/dot_general | solution.py:30
  106.5 1.8 collective-permute-start.1
  108.3 6.5 %maximum_add_fusion.3 = f32[2,1,1024,1024]{3,2,1,0:T(8,128)} fusion(f32[1,1,1024,1024]{3,2,1,0:T(8,128)S(1)} %add_bitcast_fusion.3, f32[1,1,1024,1024]{3,2,1,0:T(8,128)S(1)} %subtract_bitcast_fusion.3, f32[2,1,1024,1024]{3,2,1,0:T(8,128)} %get-tuple-element.327, pred[]{:T(512)S(6)} %compare.20), kind=kLoop, calls=%fused_computation.clone.1 | loop fusion | flops 6291456 | bytes 25165824 | tf_op jit(solution)/shard_map/while/body/eval_jaxpr/add | solution.py:34
  115.5 9.3 %all-reduce.5.cloned.1.call-done = bf16[2,1,1024,128]{3,2,1,0:T(8,128)(2,1)} async-done(((bf16[2,1,1024,128]{3,2,1,0:T(8,128)(2,1)}), bf16[2,1,1024,128]{3,2,1,0:T(8,128)(2,1)}) %all-reduce.5.cloned.1.call-update) | async-done | bytes 524304 | tf_op jit(solution)/shard_map/while/body/eval_jaxpr/psum | solution.py:14
  127.5 2.3 %dynamic-slice_select_fusion.4 = bf16[2,1,1024,128]{3,2,1,0:T(8,128)(2,1)} fusion(bf16[2,1,1024,1024]{3,2,1,0:T(8,128)(2,1)} %get-tuple-element.349, s32[]{:T(128)S(6)} %select_n.227, pred[]{:T(512)S(6)} %eq.44), kind=kLoop, calls=%fused_computation.4.clone.1 | loop fusion | flops 262144 | bytes 1048581 | tf_op jit(solution)/shard_map/while/body/eval_jaxpr/jit(_where)/select_n | solution.py:13
  131.1 1.5 collective-permute-start
  132.6 2.7 %fusion.60 = f32[1024,1024]{1,0:T(8,128)} fusion(bf16[2,1,128,1024]{3,2,1,0:T(8,128)(2,1)S(1)} %get-tuple-element.329, bf16[2,1,1024,128]{3,2,1,0:T(8,128)(2,1)S(1)} %get-tuple-element.328), kind=kOutput, calls=%fused_computation.5.clone.1 | convolution fusion | flops 268435456 | bytes 4718592 | tf_op jit(solution)/shard_map/while/body/eval_jaxpr/frk,fks->frs/dot_general | solution.py:30
  135.3 2.7 %fusion.61 = f32[1024,1024]{1,0:T(8,128)} fusion(bf16[2,1,128,1024]{3,2,1,0:T(8,128)(2,1)S(1)} %get-tuple-element.329, bf16[2,1,1024,128]{3,2,1,0:T(8,128)(2,1)S(1)} %get-tuple-element.328), kind=kOutput, calls=%fused_computation.11.clone.1 | convolution fusion | flops 268435456 | bytes 4718592 | tf_op jit(solution)/shard_map/while/body/eval_jaxpr/frk,fks->frs/dot_general | solution.py:30
  138.0 3.1 %add_bitcast_fusion.3 = f32[1,1,1024,1024]{3,2,1,0:T(8,128)S(1)} fusion(f32[1024,1024]{1,0:T(8,128)} %fusion.60, bf16[2,1,1024,128]{3,2,1,0:T(8,128)(2,1)S(1)} %get-tuple-element.328, bf16[2,1,128,1024]{3,2,1,0:T(8,128)(2,1)S(1)} %get-tuple-element.329), kind=kOutput, calls=%fused_computation.1.clone.1 | convolution fusion | flops 269484032 | bytes 8912896 | tf_op jit(solution)/shard_map/while/body/eval_jaxpr/frk,fks->frs/dot_general | solution.py:30
  145.0 1.8 collective-permute-start.1
  146.8 6.5 %maximum_add_fusion.3 = f32[2,1,1024,1024]{3,2,1,0:T(8,128)} fusion(f32[1,1,1024,1024]{3,2,1,0:T(8,128)S(1)} %add_bitcast_fusion.3, f32[1,1,1024,1024]{3,2,1,0:T(8,128)S(1)} %subtract_bitcast_fusion.3, f32[2,1,1024,1024]{3,2,1,0:T(8,128)} %get-tuple-element.327, pred[]{:T(512)S(6)} %compare.20), kind=kLoop, calls=%fused_computation.clone.1 | loop fusion | flops 6291456 | bytes 25165824 | tf_op jit(solution)/shard_map/while/body/eval_jaxpr/add | solution.py:34
  154.0 9.3 %all-reduce.5.cloned.1.call-done = bf16[2,1,1024,128]{3,2,1,0:T(8,128)(2,1)} async-done(((bf16[2,1,1024,128]{3,2,1,0:T(8,128)(2,1)}), bf16[2,1,1024,128]{3,2,1,0:T(8,128)(2,1)}) %all-reduce.5.cloned.1.call-update) | async-done | bytes 524304 | tf_op jit(solution)/shard_map/while/body/eval_jaxpr/psum | solution.py:14
  167.5 4.7 %maximum_add_fusion.1 = f32[2,1,1024,1024]{3,2,1,0:T(8,128)S(1)} fusion(f32[2,1,1024,1024]{3,2,1,0:T(8,128)} %get-tuple-element.209, f32[1,1,1024,1024]{3,2,1,0:T(8,128)S(1)} %add_bitcast_fusion.1, f32[1,1,1024,1024]{3,2,1,0:T(8,128)S(1)} %subtract_bitcast_fusion.1), kind=kLoop, calls=%fused_computation.25 | loop fusion | flops 4194304 | bytes 25165824 | tf_op jit(solution)/shard_map/add | solution.py:34
  172.2 2.6 %fusion.18 = (bf16[1,1,1,1024,1024]{4,3,2,1,0:T(8,128)(2,1)S(1)}, bf16[1,1,1,1024,1024]{4,3,2,1,0:T(8,128)(2,1)S(1)}) fusion(f32[2,1,1024,1024]{3,2,1,0:T(8,128)S(1)} %maximum_add_fusion.1, f32[]{:T(128)} %bitcast.13, f32[]{:T(128)} %bitcast), kind=kLoop, calls=%fused_computation.31 | loop fusion | flops 10485760 | bytes 12582920 | tf_op jit(solution)/shard_map/stack | solution.py:89
  174.9 2.4 %pad_maximum_fusion = bf16[2,1,1,1024,1024]{4,3,2,1,0:T(8,128)(2,1)} fusion(bf16[1,1,1,1024,1024]{4,3,2,1,0:T(8,128)(2,1)S(1)} %get-tuple-element.256, bf16[1,1,1,1024,1024]{4,3,2,1,0:T(8,128)(2,1)S(1)} %get-tuple-element.255), kind=kLoop, calls=%fused_computation.26 | loop fusion | flops 2097152 | bytes 8388608 | tf_op jit(solution)/shard_map/stack | solution.py:89
  (61 shorter events, 33.1 us)
Async XLA Ops:
  6.5 21.0 %copy-start = (f32[2,2]{1,0:T(2,128)S(1)}, f32[2,2]{1,0:T(2,128)}, u32[]{:S(2)}) copy-start(f32[2,2]{1,0:T(2,128)} %param.9) | copy-start | bytes 52
  6.5 42.5 %copy-start.3 = (s32[32]{0:T(128)S(1)}, s32[32]{0:T(128)}, u32[]{:S(2)}) copy-start(s32[32]{0:T(128)} %param.8) | copy-start | bytes 388
  6.5 41.2 %all-reduce.3.cloned.1.call-start = ((), (), s32[]{:S(2)}) async-start(), calls=%async_computation | async-start | bytes 1048576 | tf_op jit(solution)/shard_map/psum | solution.py:14
  8.5 15.0 %collective-permute-start.2 = (bf16[2,1,128,1024]{3,2,1,0:T(8,128)(2,1)S(1)}, bf16[2,1,128,1024]{3,2,1,0:T(8,128)(2,1)S(1)}, u32[]{:S(2)}, u32[]{:S(2)}) collective-permute-start(bf16[2,1,128,1024]{3,2,1,0:T(8,128)(2,1)S(1)} %select_bitcast_fusion), channel_id=1, source_target_pairs={{0,1},{1,0},{2,3},{3,2},{4,5},{5,4},{6,7},{7,6},{8,9},{9,8},{10,11... | collective-permute-start | bytes 1572872 | tf_op jit(solution)/shard_map/ppermute | solution.py:24
  24.8 24.0 %collective-permute-start.3 = (bf16[2,1,128,1024]{3,2,1,0:T(8,128)(2,1)S(1)}, bf16[2,1,128,1024]{3,2,1,0:T(8,128)(2,1)S(1)}, u32[]{:S(2)}, u32[]{:S(2)}) collective-permute-start(bf16[2,1,128,1024]{3,2,1,0:T(8,128)(2,1)S(1)} %fusion.40), channel_id=1, source_target_pairs={{0,2},{2,0},{1,3},{3,1},{4,6},{6,4},{5,7},{7,5},{8,10},{10,8},{9,1... | collective-permute-start | bytes 1572872 | tf_op jit(solution)/shard_map/ppermute | solution.py:24
  49.1 37.3 %all-reduce.5.cloned.1.call-start = ((), (), s32[]{:S(2)}) async-start(), calls=%async_computation.1 | async-start | bytes 1048576 | tf_op jit(solution)/shard_map/while/body/eval_jaxpr/psum | solution.py:14
  54.0 12.5 %collective-permute-start = (bf16[2,1,128,1024]{3,2,1,0:T(8,128)(2,1)S(1)}, bf16[2,1,128,1024]{3,2,1,0:T(8,128)(2,1)S(1)}, u32[]{:S(2)}, u32[]{:S(2)}) collective-permute-start(bf16[2,1,128,1024]{3,2,1,0:T(8,128)(2,1)S(1)} %dynamic-slice_select_fusion.5), channel_id=1, source_target_pairs={{0,1},{1,0},{2,3},{3,2},{4,5},{5,4},{6,7},{7,6},{8,9},{9,8},{10,11... | collective-permute-start | bytes 1572872 | tf_op jit(solution)/shard_map/while/body/eval_jaxpr/ppermute | solution.py:24
  60.9 3.5 %copy-start.2 = (f32[1024,1024]{1,0:T(8,128)S(1)}, f32[1024,1024]{1,0:T(8,128)}, u32[]{:S(2)}) copy-start(f32[1024,1024]{1,0:T(8,128)} %fusion.61) | copy-start | bytes 12582916 | tf_op jit(solution)/shard_map/while
  67.8 19.6 %collective-permute-start.1 = (bf16[2,1,128,1024]{3,2,1,0:T(8,128)(2,1)S(1)}, bf16[2,1,128,1024]{3,2,1,0:T(8,128)(2,1)S(1)}, u32[]{:S(2)}, u32[]{:S(2)}) collective-permute-start(bf16[2,1,128,1024]{3,2,1,0:T(8,128)(2,1)S(1)} %fusion.62), channel_id=1, source_target_pairs={{0,2},{2,0},{1,3},{3,1},{4,6},{6,4},{5,7},{7,5},{8,10},{10,8},{9,1... | collective-permute-start | bytes 1572872 | tf_op jit(solution)/shard_map/while/body/eval_jaxpr/ppermute | solution.py:24
  87.7 37.2 %all-reduce.5.cloned.1.call-start = ((), (), s32[]{:S(2)}) async-start(), calls=%async_computation.1 | async-start | bytes 1048576 | tf_op jit(solution)/shard_map/while/body/eval_jaxpr/psum | solution.py:14
  92.6 12.6 %collective-permute-start = (bf16[2,1,128,1024]{3,2,1,0:T(8,128)(2,1)S(1)}, bf16[2,1,128,1024]{3,2,1,0:T(8,128)(2,1)S(1)}, u32[]{:S(2)}, u32[]{:S(2)}) collective-permute-start(bf16[2,1,128,1024]{3,2,1,0:T(8,128)(2,1)S(1)} %dynamic-slice_select_fusion.5), channel_id=1, source_target_pairs={{0,1},{1,0},{2,3},{3,2},{4,5},{5,4},{6,7},{7,6},{8,9},{9,8},{10,11... | collective-permute-start | bytes 1572872 | tf_op jit(solution)/shard_map/while/body/eval_jaxpr/ppermute | solution.py:24
  99.4 3.5 %copy-start.2 = (f32[1024,1024]{1,0:T(8,128)S(1)}, f32[1024,1024]{1,0:T(8,128)}, u32[]{:S(2)}) copy-start(f32[1024,1024]{1,0:T(8,128)} %fusion.61) | copy-start | bytes 12582916 | tf_op jit(solution)/shard_map/while
  106.5 19.5 %collective-permute-start.1 = (bf16[2,1,128,1024]{3,2,1,0:T(8,128)(2,1)S(1)}, bf16[2,1,128,1024]{3,2,1,0:T(8,128)(2,1)S(1)}, u32[]{:S(2)}, u32[]{:S(2)}) collective-permute-start(bf16[2,1,128,1024]{3,2,1,0:T(8,128)(2,1)S(1)} %fusion.62), channel_id=1, source_target_pairs={{0,2},{2,0},{1,3},{3,1},{4,6},{6,4},{5,7},{7,5},{8,10},{10,8},{9,1... | collective-permute-start | bytes 1572872 | tf_op jit(solution)/shard_map/while/body/eval_jaxpr/ppermute | solution.py:24
  126.2 37.2 %all-reduce.5.cloned.1.call-start = ((), (), s32[]{:S(2)}) async-start(), calls=%async_computation.1 | async-start | bytes 1048576 | tf_op jit(solution)/shard_map/while/body/eval_jaxpr/psum | solution.py:14
  131.1 12.6 %collective-permute-start = (bf16[2,1,128,1024]{3,2,1,0:T(8,128)(2,1)S(1)}, bf16[2,1,128,1024]{3,2,1,0:T(8,128)(2,1)S(1)}, u32[]{:S(2)}, u32[]{:S(2)}) collective-permute-start(bf16[2,1,128,1024]{3,2,1,0:T(8,128)(2,1)S(1)} %dynamic-slice_select_fusion.5), channel_id=1, source_target_pairs={{0,1},{1,0},{2,3},{3,2},{4,5},{5,4},{6,7},{7,6},{8,9},{9,8},{10,11... | collective-permute-start | bytes 1572872 | tf_op jit(solution)/shard_map/while/body/eval_jaxpr/ppermute | solution.py:24
  138.0 3.5 %copy-start.2 = (f32[1024,1024]{1,0:T(8,128)S(1)}, f32[1024,1024]{1,0:T(8,128)}, u32[]{:S(2)}) copy-start(f32[1024,1024]{1,0:T(8,128)} %fusion.61) | copy-start | bytes 12582916 | tf_op jit(solution)/shard_map/while
  145.0 19.5 %collective-permute-start.1 = (bf16[2,1,128,1024]{3,2,1,0:T(8,128)(2,1)S(1)}, bf16[2,1,128,1024]{3,2,1,0:T(8,128)(2,1)S(1)}, u32[]{:S(2)}, u32[]{:S(2)}) collective-permute-start(bf16[2,1,128,1024]{3,2,1,0:T(8,128)(2,1)S(1)} %fusion.62), channel_id=1, source_target_pairs={{0,2},{2,0},{1,3},{3,1},{4,6},{6,4},{5,7},{7,5},{8,10},{10,8},{9,1... | collective-permute-start | bytes 1572872 | tf_op jit(solution)/shard_map/while/body/eval_jaxpr/ppermute | solution.py:24
  174.9 2.4 %copy-start.1 = (f32[2,2]{1,0:T(2,128)S(1)}, f32[2,2]{1,0:T(2,128)}, u32[]{:S(2)}) copy-start(f32[2,2]{1,0:T(2,128)} %param.9) | copy-start | bytes 52
Sparse Core Ops, SparseCore 0:
  14.0 33.7 all-reduce.2
  52.9 33.4 all-reduce.4
  91.4 33.3 all-reduce.4
  130.0 33.3 all-reduce.4
where the time goes:
time: 185 us; the launch traced here: 184 us
  waiting for transfers between devices  64.2 us (35%)
  other arithmetic  54.4 us (29%)
  matrix products  30.1 us (16%)
  starting transfers between devices  15.1 us (8%)
  between operations  14 us (8%)
  local copies, waits for them, and re-layouts  3.74 us (2%)
  loops' own time  2.35 us (1%)
    psum x4, waiting for transfers between devices, spread(): return lax.psum(block, axis)  50.1 us
    dot_general x16, matrix products, product(): jnp.einsum('frk,fks->frs', first, second, preferred_element_type=jnp.floa...  30.1 us
    add x4, other arithmetic, accumulate(): return total + jnp.stack([real, imag])  21.9 us
    ppermute x8, starting transfers between devices, partner(): return lax.ppermute(block, axis, route)  15 us
    ppermute x8, waiting for transfers between devices, partner(): return lax.ppermute(block, axis, route)  14 us
    select_n x4, other arithmetic, spread(): jnp.where(lax.axis_index(axis) == holder, block, jnp.zeros_like(block))  9.12 us
    add x8, other arithmetic, rows_of(): value = value + partner(value, 'recv', bit)  6.04 us
    another operation x2, other arithmetic, shards(): result = jnp.stack([out_re, out_im]).astype(jnp.bfloat16)  5.02 us
  transfers between devices with their start and end apart: 12, of which 8 were waited for; matrix products, arithmetic and copies ran while one was open for 35% of the time, Pallas kernels for 0%

commit v1 on v0

--- a/solution.py
+++ b/solution.py
@@ -11,7 +11,10 @@
 
 def spread(block, axis, holder):
     block = jnp.where(lax.axis_index(axis) == holder, block, jnp.zeros_like(block))
-    return lax.psum(block, axis)
+    recast_lane = lambda unit, comm_axis: jnp.sum(
+        jax.lax.all_gather(unit, axis_name=comm_axis), axis=0
+    )
+    return recast_lane(block, axis)
 
 
 def partner(block, axis, apart):

time: 185 us -> 162 us (0.88)
  matrix products: 30.1 us -> 13.3 us
  local copies, waits for them, and re-layouts: 3.74 us -> 13.7 us
  waiting for transfers between devices: 64.2 us -> 55.9 us
  other arithmetic: 54.4 us -> 47.5 us
    psum x4 -> x0, waiting for transfers between devices: 50.1 us -> none  [spread(): return lax.psum(block, axis)]
    ppermute x8, waiting for transfers between devices: 14 us -> 55.8 us  [partner(): return lax.ppermute(block, axis, route)]
    dot_general x16, matrix products: 30.1 us -> 13.3 us  [product(): jnp.einsum('frk,fks->frs', first, second, preferred_element_type=jnp.floa...]
    add x4, other arithmetic: 21.9 us -> 11.5 us  [accumulate(): return total + jnp.stack([real, imag])]
    while x6 -> x18, local copies, waits for them, and re-layouts: 1.29 us -> 9.72 us
    reduce_sum x0 -> x4, other arithmetic: none -> 7.75 us  [spread(): jnp.sum(jax.lax.all_gather(unit, axis_name=comm_axis), axis=0)]
    mul x4, other arithmetic: 4.31 us -> 0.16 us  [columns_of(): return columns * weight[None, None, None, :]]
  transfers between devices with their start and end apart: 12 -> 12, of which waited for: 8 -> 8; matrix products, arithmetic and copies ran while one was open for 35% -> 19% of each run, Pallas kernels for 0% -> 0%
where the time goes in v1:
time: 162 us; the launch traced here: 161 us
  waiting for transfers between devices  55.9 us (35%)
  other arithmetic  47.5 us (29%)
  between operations  13.9 us (9%)
  starting transfers between devices  13.8 us (9%)
  local copies, waits for them, and re-layouts  13.7 us (8%)
  matrix products  13.3 us (8%)
  loops' own time  2.47 us (2%)
    ppermute x8, waiting for transfers between devices, partner(): return lax.ppermute(block, axis, route)  55.8 us
    ppermute x8, starting transfers between devices, partner(): return lax.ppermute(block, axis, route)  13.7 us
    dot_general x16, matrix products, product(): jnp.einsum('frk,fks->frs', first, second, preferred_element_type=jnp.floa...  13.3 us
    add x4, other arithmetic, accumulate(): return total + jnp.stack([real, imag])  11.5 us
    while x18, local copies, waits for them, and re-layouts  9.72 us
    select_n x4, other arithmetic, spread(): jnp.where(lax.axis_index(axis) == holder, block, jnp.zeros_like(block))  9.07 us
    reduce_sum x4, other arithmetic, spread(): jnp.sum(jax.lax.all_gather(unit, axis_name=comm_axis), axis=0)  7.75 us
    add x8, other arithmetic, rows_of(): value = value + partner(value, 'recv', bit)  6.04 us
  transfers between devices with their start and end apart: 12, of which 8 were waited for; matrix products, arithmetic and copies ran while one was open for 19% of the time, Pallas kernels for 0%

profile of v1, /device:TPU:0, one launch (start us, length us, event | category | flops | bytes accessed | tf_op | source)
XLA Modules:
  0.0 160.6 jit_solution(237408483377770300)
XLA Ops:
  7.2 2.3 %dynamic-slice_select_fusion.2 = bf16[2,1,1,1024,128]{4,3,2,1,0:T(8,128)(2,1)} fusion(bf16[2,1,1,1024,1024]{4,3,2,1,0:T(8,128)(2,1)} %param.6, s32[]{:T(128)S(6)} %select_n.176, pred[]{:T(512)S(6)} %eq.38), kind=kLoop, calls=%fused_computation.36 | loop fusion | flops 262144 | bytes 1048581 | tf_op jit(solution)/shard_map/jit(_where)/select_n | solution.py:13
  10.8 3.0 %collective-permute-start.2 = (bf16[2,1,128,1024]{3,2,1,0:T(8,128)(2,1)S(1)}, bf16[2,1,128,1024]{3,2,1,0:T(8,128)(2,1)S(1)}, u32[]{:S(2)}, u32[]{:S(2)}) collective-permute-start(bf16[2,1,128,1024]{3,2,1,0:T(8,128)(2,1)S(1)} %select_bitcast_fusion), channel_id=1, source_target_pairs={{0,1},{1,0},{2,3},{3,2},{4,5},{5,4},{6,7},{7,6},{8,9},{9,8},{10,11... | collective-permute-start | bytes 1572872 | tf_op jit(solution)/shard_map/ppermute | solution.py:27
  13.8 11.9 %collective-permute-done.2 = bf16[2,1,128,1024]{3,2,1,0:T(8,128)(2,1)S(1)} collective-permute-done((bf16[2,1,128,1024]{3,2,1,0:T(8,128)(2,1)S(1)}, bf16[2,1,128,1024]{3,2,1,0:T(8,128)(2,1)S(1)}, u32[]{:S(2)}, u32[]{:S(2)}) %collective-permute-start.2) | collective-permute-done | bytes 524320 | tf_op jit(solution)/shard_map/ppermute | solution.py:27
  27.1 1.9 %collective-permute-start.3 = (bf16[2,1,128,1024]{3,2,1,0:T(8,128)(2,1)S(1)}, bf16[2,1,128,1024]{3,2,1,0:T(8,128)(2,1)S(1)}, u32[]{:S(2)}, u32[]{:S(2)}) collective-permute-start(bf16[2,1,128,1024]{3,2,1,0:T(8,128)(2,1)S(1)} %fusion.40), channel_id=1, source_target_pairs={{0,2},{2,0},{1,3},{3,1},{4,6},{6,4},{5,7},{7,5},{8,10},{10,8},{9,1... | collective-permute-start | bytes 1572872 | tf_op jit(solution)/shard_map/ppermute | solution.py:27
  30.3 10.0 %collective-permute-done.3 = bf16[2,1,128,1024]{3,2,1,0:T(8,128)(2,1)S(1)} collective-permute-done((bf16[2,1,128,1024]{3,2,1,0:T(8,128)(2,1)S(1)}, bf16[2,1,128,1024]{3,2,1,0:T(8,128)(2,1)S(1)}, u32[]{:S(2)}, u32[]{:S(2)}) %collective-permute-start.3) | collective-permute-done | bytes 524320 | tf_op jit(solution)/shard_map/ppermute | solution.py:27
  40.6 2.1 %reduce.10 = bf16[2,1024,128]{2,1,0:T(8,128)(2,1)S(1)} reduce(bf16[4,2,1024,128]{3,2,1,0:T(8,128)(2,1)} %bitcast.105, bf16[]{:T(256)} %constant.206.clone.1), dimensions={0}, to_apply=%region_0.1 | reduce | flops 786432 | bytes 2621442 | tf_op jit(solution)/shard_map/reduce_sum | solution.py:14
  42.7 95.9 %while.20 = (s32[]{:T(128)}, f32[2,1,1024,1024]{3,2,1,0:T(8,128)}, bf16[2,1,1024,128]{3,2,0,1:T(8,128)(2,1)S(1)}, bf16[2,1,128,1024]{3,2,1,0:T(8,128)(2,1)S(1)},...) while((s32[]{:T(128)}, f32[2,1,1024,1024]{3,2,1,0:T(8,128)}, ...), condition=%wide.region_3.4_spmd.clone, body=%wide.region_1.3_spmd.clone.sunk | while | flops 1085276288 | bytes 132122368 | solution.py:86
  44.1 2.3 %dynamic-slice_select_fusion.5 = bf16[2,1,1024,128]{3,2,1,0:T(8,128)(2,1)} fusion(bf16[2,1,1024,1024]{3,2,1,0:T(8,128)(2,1)} %get-tuple-element.350, s32[]{:T(128)S(6)} %select_n.228, pred[]{:T(512)S(6)} %eq.44), kind=kLoop, calls=%fused_computation.6.clone.1 | loop fusion | flops 262144 | bytes 1048581 | tf_op jit(solution)/shard_map/while/body/eval_jaxpr/jit(_where)/select_n | solution.py:13
  52.7 7.3 %collective-permute-done = bf16[2,1,128,1024]{3,2,1,0:T(8,128)(2,1)S(1)} collective-permute-done((bf16[2,1,128,1024]{3,2,1,0:T(8,128)(2,1)S(1)}, bf16[2,1,128,1024]{3,2,1,0:T(8,128)(2,1)S(1)}, u32[]{:S(2)}, u32[]{:S(2)}) %collective-permute-start) | collective-permute-done | bytes 524320 | tf_op jit(solution)/shard_map/while/body/eval_jaxpr/ppermute | solution.py:27
  62.6 2.5 %maximum_add_fusion.3 = f32[2,1,1024,1024]{3,2,1,0:T(8,128)S(1)} fusion(f32[1,1,1024,1024]{3,2,1,0:T(8,128)S(1)} %add_bitcast_fusion.3, f32[1,1,1024,1024]{3,2,1,0:T(8,128)S(1)} %subtract_bitcast_fusion.3, f32[2,1,1024,1024]{3,2,1,0:T(8,128)S(1)} %bitcast.98, pred[]{:T(512)S(6)} %compare.20), kind=kLoop, calls=%fused_computation.clone.1 | loop fusion | flops 6291456 | bytes 25165824 | tf_op jit(solution)/shard_map/while/body/eval_jaxpr/add | solution.py:37
  65.2 3.2 %copy-done.2 = f32[2,1,1024,1024]{3,2,1,0:T(8,128)} copy-done((f32[2,1,1024,1024]{3,2,1,0:T(8,128)}, f32[2,1,1024,1024]{3,2,1,0:T(8,128)S(1)}, u32[]{:S(2)}) %copy-start.2) | copy-done | bytes 8388632 | tf_op jit(solution)/shard_map/while
  68.4 4.4 %collective-permute-done.1 = bf16[2,1,128,1024]{3,2,1,0:T(8,128)(2,1)S(1)} collective-permute-done((bf16[2,1,128,1024]{3,2,1,0:T(8,128)(2,1)S(1)}, bf16[2,1,128,1024]{3,2,1,0:T(8,128)(2,1)S(1)}, u32[]{:S(2)}, u32[]{:S(2)}) %collective-permute-start.1) | collective-permute-done | bytes 524320 | tf_op jit(solution)/shard_map/while/body/eval_jaxpr/ppermute | solution.py:27
  73.1 1.9 %bitcast_reduce_fusion.2 = bf16[2,1024,128]{2,1,0:T(8,128)(2,1)S(1)} fusion(bf16[4,2,1024,128]{3,2,1,0:T(8,128)(2,1)} %bitcast.101), kind=kLoop, calls=%fused_computation.3.clone.1 | loop fusion | flops 786432 | bytes 2621440 | tf_op jit(solution)/shard_map/while/body/eval_jaxpr/reduce_sum | solution.py:14
  76.4 2.3 %dynamic-slice_select_fusion.5 = bf16[2,1,1024,128]{3,2,1,0:T(8,128)(2,1)} fusion(bf16[2,1,1024,1024]{3,2,1,0:T(8,128)(2,1)} %get-tuple-element.350, s32[]{:T(128)S(6)} %select_n.228, pred[]{:T(512)S(6)} %eq.44), kind=kLoop, calls=%fused_computation.6.clone.1 | loop fusion | flops 262144 | bytes 1048581 | tf_op jit(solution)/shard_map/while/body/eval_jaxpr/jit(_where)/select_n | solution.py:13
  84.5 6.7 %collective-permute-done = bf16[2,1,128,1024]{3,2,1,0:T(8,128)(2,1)S(1)} collective-permute-done((bf16[2,1,128,1024]{3,2,1,0:T(8,128)(2,1)S(1)}, bf16[2,1,128,1024]{3,2,1,0:T(8,128)(2,1)S(1)}, u32[]{:S(2)}, u32[]{:S(2)}) %collective-permute-start) | collective-permute-done | bytes 524320 | tf_op jit(solution)/shard_map/while/body/eval_jaxpr/ppermute | solution.py:27
  92.5 1.6 collective-permute-start.1
  94.1 2.5 %maximum_add_fusion.3 = f32[2,1,1024,1024]{3,2,1,0:T(8,128)S(1)} fusion(f32[1,1,1024,1024]{3,2,1,0:T(8,128)S(1)} %add_bitcast_fusion.3, f32[1,1,1024,1024]{3,2,1,0:T(8,128)S(1)} %subtract_bitcast_fusion.3, f32[2,1,1024,1024]{3,2,1,0:T(8,128)S(1)} %bitcast.98, pred[]{:T(512)S(6)} %compare.20), kind=kLoop, calls=%fused_computation.clone.1 | loop fusion | flops 6291456 | bytes 25165824 | tf_op jit(solution)/shard_map/while/body/eval_jaxpr/add | solution.py:37
  96.7 3.2 %copy-done.2 = f32[2,1,1024,1024]{3,2,1,0:T(8,128)} copy-done((f32[2,1,1024,1024]{3,2,1,0:T(8,128)}, f32[2,1,1024,1024]{3,2,1,0:T(8,128)S(1)}, u32[]{:S(2)}) %copy-start.2) | copy-done | bytes 8388632 | tf_op jit(solution)/shard_map/while
  99.9 3.4 %collective-permute-done.1 = bf16[2,1,128,1024]{3,2,1,0:T(8,128)(2,1)S(1)} collective-permute-done((bf16[2,1,128,1024]{3,2,1,0:T(8,128)(2,1)S(1)}, bf16[2,1,128,1024]{3,2,1,0:T(8,128)(2,1)S(1)}, u32[]{:S(2)}, u32[]{:S(2)}) %collective-permute-start.1) | collective-permute-done | bytes 524320 | tf_op jit(solution)/shard_map/while/body/eval_jaxpr/ppermute | solution.py:27
  103.5 1.9 %bitcast_reduce_fusion.2 = bf16[2,1024,128]{2,1,0:T(8,128)(2,1)S(1)} fusion(bf16[4,2,1024,128]{3,2,1,0:T(8,128)(2,1)} %bitcast.101), kind=kLoop, calls=%fused_computation.3.clone.1 | loop fusion | flops 786432 | bytes 2621440 | tf_op jit(solution)/shard_map/while/body/eval_jaxpr/reduce_sum | solution.py:14
  106.8 2.3 %dynamic-slice_select_fusion.5 = bf16[2,1,1024,128]{3,2,1,0:T(8,128)(2,1)} fusion(bf16[2,1,1024,1024]{3,2,1,0:T(8,128)(2,1)} %get-tuple-element.350, s32[]{:T(128)S(6)} %select_n.228, pred[]{:T(512)S(6)} %eq.44), kind=kLoop, calls=%fused_computation.6.clone.1 | loop fusion | flops 262144 | bytes 1048581 | tf_op jit(solution)/shard_map/while/body/eval_jaxpr/jit(_where)/select_n | solution.py:13
  110.3 1.8 %collective-permute-start = (bf16[2,1,128,1024]{3,2,1,0:T(8,128)(2,1)S(1)}, bf16[2,1,128,1024]{3,2,1,0:T(8,128)(2,1)S(1)}, u32[]{:S(2)}, u32[]{:S(2)}) collective-permute-start(bf16[2,1,128,1024]{3,2,1,0:T(8,128)(2,1)S(1)} %dynamic-slice_select_fusion.6), channel_id=1, source_target_pairs={{0,1},{1,0},{2,3},{3,2},{4,5},{5,4},{6,7},{7,6},{8,9},{9,8},{10,11... | collective-permute-start | bytes 1572872 | tf_op jit(solution)/shard_map/while/body/eval_jaxpr/ppermute | solution.py:27
  115.7 7.4 %collective-permute-done = bf16[2,1,128,1024]{3,2,1,0:T(8,128)(2,1)S(1)} collective-permute-done((bf16[2,1,128,1024]{3,2,1,0:T(8,128)(2,1)S(1)}, bf16[2,1,128,1024]{3,2,1,0:T(8,128)(2,1)S(1)}, u32[]{:S(2)}, u32[]{:S(2)}) %collective-permute-start) | collective-permute-done | bytes 524320 | tf_op jit(solution)/shard_map/while/body/eval_jaxpr/ppermute | solution.py:27
  126.0 2.5 %maximum_add_fusion.3 = f32[2,1,1024,1024]{3,2,1,0:T(8,128)S(1)} fusion(f32[1,1,1024,1024]{3,2,1,0:T(8,128)S(1)} %add_bitcast_fusion.3, f32[1,1,1024,1024]{3,2,1,0:T(8,128)S(1)} %subtract_bitcast_fusion.3, f32[2,1,1024,1024]{3,2,1,0:T(8,128)S(1)} %bitcast.98, pred[]{:T(512)S(6)} %compare.20), kind=kLoop, calls=%fused_computation.clone.1 | loop fusion | flops 6291456 | bytes 25165824 | tf_op jit(solution)/shard_map/while/body/eval_jaxpr/add | solution.py:37
  128.5 3.2 %copy-done.2 = f32[2,1,1024,1024]{3,2,1,0:T(8,128)} copy-done((f32[2,1,1024,1024]{3,2,1,0:T(8,128)}, f32[2,1,1024,1024]{3,2,1,0:T(8,128)S(1)}, u32[]{:S(2)}) %copy-start.2) | copy-done | bytes 8388632 | tf_op jit(solution)/shard_map/while
  131.8 4.7 %collective-permute-done.1 = bf16[2,1,128,1024]{3,2,1,0:T(8,128)(2,1)S(1)} collective-permute-done((bf16[2,1,128,1024]{3,2,1,0:T(8,128)(2,1)S(1)}, bf16[2,1,128,1024]{3,2,1,0:T(8,128)(2,1)S(1)}, u32[]{:S(2)}, u32[]{:S(2)}) %collective-permute-start.1) | collective-permute-done | bytes 524320 | tf_op jit(solution)/shard_map/while/body/eval_jaxpr/ppermute | solution.py:27
  136.7 1.9 %bitcast_reduce_fusion.2 = bf16[2,1024,128]{2,1,0:T(8,128)(2,1)S(1)} fusion(bf16[4,2,1024,128]{3,2,1,0:T(8,128)(2,1)} %bitcast.101), kind=kLoop, calls=%fused_computation.3.clone.1 | loop fusion | flops 786432 | bytes 2621440 | tf_op jit(solution)/shard_map/while/body/eval_jaxpr/reduce_sum | solution.py:14
  140.7 2.8 %subtract_bitcast_fusion.1 = f32[1,1,1024,1024]{3,2,1,0:T(8,128)} fusion(f32[1024,1024]{1,0:T(8,128)S(1)} %fusion.26, bf16[2,1,128,1024]{3,2,1,0:T(8,128)(2,1)S(1)} %get-tuple-element.212, bf16[2,1,1024,128]{3,2,0,1:T(8,128)(2,1)S(1)} %get-tuple-element.211), kind=kOutput, calls=%fused_computation.31 | convolution fusion | flops 269484032 | bytes 8912896 | tf_op jit(solution)/shard_map/frk,fks->frs/dot_general | solution.py:33
  143.6 1.6 %slice-done.3 = s8[4194304]{0:T(1024)(128)(4,1)S(1)} async-done(((s8[8388608]{0:T(1024)(128)(4,1)}), s8[4194304]{0:T(1024)(128)(4,1)S(1)}, s32[]{:S(2)}) %slice-start.3) | async-done | bytes 4194328
  145.2 3.9 %maximum_add_fusion.1 = f32[2,1,1024,1024]{3,2,1,0:T(8,128)S(1)} fusion(f32[2,1,1024,1024]{3,2,1,0:T(8,128)S(1)} %bitcast.100, f32[1,1,1024,1024]{3,2,1,0:T(8,128)S(1)} %add_bitcast_fusion.1, f32[1,1,1024,1024]{3,2,1,0:T(8,128)} %subtract_bitcast_fusion.1), kind=kLoop, calls=%fused_computation.26 | loop fusion | flops 4194304 | bytes 25165824 | tf_op jit(solution)/shard_map/add | solution.py:37
  149.1 2.6 %fusion.18 = (bf16[1,1,1,1024,1024]{4,3,2,1,0:T(8,128)(2,1)S(1)}, bf16[1,1,1,1024,1024]{4,3,2,1,0:T(8,128)(2,1)S(1)}) fusion(f32[2,1,1024,1024]{3,2,1,0:T(8,128)S(1)} %maximum_add_fusion.1, f32[]{:T(128)} %bitcast.13, f32[]{:T(128)} %bitcast), kind=kLoop, calls=%fused_computation.32 | loop fusion | flops 10485760 | bytes 12582920 | tf_op jit(solution)/shard_map/stack | solution.py:92
  151.7 2.4 %pad_maximum_fusion = bf16[2,1,1,1024,1024]{4,3,2,1,0:T(8,128)(2,1)} fusion(bf16[1,1,1,1024,1024]{4,3,2,1,0:T(8,128)(2,1)S(1)} %get-tuple-element.257, bf16[1,1,1,1024,1024]{4,3,2,1,0:T(8,128)(2,1)S(1)} %get-tuple-element.256), kind=kLoop, calls=%fused_computation.27 | loop fusion | flops 2097152 | bytes 8388608 | tf_op jit(solution)/shard_map/stack | solution.py:92
  (85 shorter events, 32.8 us)
Async XLA Ops:
  6.5 23.2 %copy-start = (f32[2,2]{1,0:T(2,128)S(1)}, f32[2,2]{1,0:T(2,128)}, u32[]{:S(2)}) copy-start(f32[2,2]{1,0:T(2,128)} %param.9) | copy-start | bytes 52
  6.5 34.0 %all-gather.8.cloned.1.call-start = ((), (), s32[]{:S(2)}) async-start(), calls=%async_computation | async-start | bytes 2621440 | tf_op jit(solution)/shard_map/all_gather | solution.py:15
  9.5 33.2 %copy-start.3 = (s32[32]{0:T(128)S(1)}, s32[32]{0:T(128)}, u32[]{:S(2)}) copy-start(s32[32]{0:T(128)} %param.8) | copy-start | bytes 388
  10.8 15.0 %collective-permute-start.2 = (bf16[2,1,128,1024]{3,2,1,0:T(8,128)(2,1)S(1)}, bf16[2,1,128,1024]{3,2,1,0:T(8,128)(2,1)S(1)}, u32[]{:S(2)}, u32[]{:S(2)}) collective-permute-start(bf16[2,1,128,1024]{3,2,1,0:T(8,128)(2,1)S(1)} %select_bitcast_fusion), channel_id=1, source_target_pairs={{0,1},{1,0},{2,3},{3,2},{4,5},{5,4},{6,7},{7,6},{8,9},{9,8},{10,11... | collective-permute-start | bytes 1572872 | tf_op jit(solution)/shard_map/ppermute | solution.py:27
  27.1 13.3 %collective-permute-start.3 = (bf16[2,1,128,1024]{3,2,1,0:T(8,128)(2,1)S(1)}, bf16[2,1,128,1024]{3,2,1,0:T(8,128)(2,1)S(1)}, u32[]{:S(2)}, u32[]{:S(2)}) collective-permute-start(bf16[2,1,128,1024]{3,2,1,0:T(8,128)(2,1)S(1)} %fusion.40), channel_id=1, source_target_pairs={{0,2},{2,0},{1,3},{3,1},{4,6},{6,4},{5,7},{7,5},{8,10},{10,8},{9,1... | collective-permute-start | bytes 1572872 | tf_op jit(solution)/shard_map/ppermute | solution.py:27
  42.7 30.3 %all-gather.10.cloned.1.call-start = ((), (), s32[]{:S(2)}) async-start(), calls=%async_computation.1 | async-start | bytes 2621440 | tf_op jit(solution)/shard_map/while/body/eval_jaxpr/all_gather | solution.py:15
  47.6 12.4 %collective-permute-start = (bf16[2,1,128,1024]{3,2,1,0:T(8,128)(2,1)S(1)}, bf16[2,1,128,1024]{3,2,1,0:T(8,128)(2,1)S(1)}, u32[]{:S(2)}, u32[]{:S(2)}) collective-permute-start(bf16[2,1,128,1024]{3,2,1,0:T(8,128)(2,1)S(1)} %dynamic-slice_select_fusion.6), channel_id=1, source_target_pairs={{0,1},{1,0},{2,3},{3,2},{4,5},{5,4},{6,7},{7,6},{8,9},{9,8},{10,11... | collective-permute-start | bytes 1572872 | tf_op jit(solution)/shard_map/while/body/eval_jaxpr/ppermute | solution.py:27
  51.3 11.3 %slice-start = ((s8[8388608]{0:T(1024)(128)(4,1)}), s8[4194304]{0:T(1024)(128)(4,1)S(1)}, s32[]{:S(2)}) async-start(s8[8388608]{0:T(1024)(128)(4,1)} %bitcast.97), calls=%async_computation.2 | async-start | bytes 8388608 | tf_op jit(solution)/shard_map/while
  52.0 10.6 %slice-start.1 = ((s8[8388608]{0:T(1024)(128)(4,1)}), s8[4194304]{0:T(1024)(128)(4,1)S(1)}, s32[]{:S(2)}) async-start(s8[8388608]{0:T(1024)(128)(4,1)} %bitcast.97), calls=%async_computation.3 | async-start | bytes 8388608 | tf_op jit(solution)/shard_map/while
  61.3 11.5 %collective-permute-start.1 = (bf16[2,1,128,1024]{3,2,1,0:T(8,128)(2,1)S(1)}, bf16[2,1,128,1024]{3,2,1,0:T(8,128)(2,1)S(1)}, u32[]{:S(2)}, u32[]{:S(2)}) collective-permute-start(bf16[2,1,128,1024]{3,2,1,0:T(8,128)(2,1)S(1)} %fusion.62), channel_id=1, source_target_pairs={{0,2},{2,0},{1,3},{3,1},{4,6},{6,4},{5,7},{7,5},{8,10},{10,8},{9,1... | collective-permute-start | bytes 1572872 | tf_op jit(solution)/shard_map/while/body/eval_jaxpr/ppermute | solution.py:27
  65.2 3.2 %copy-start.2 = (f32[2,1,1024,1024]{3,2,1,0:T(8,128)}, f32[2,1,1024,1024]{3,2,1,0:T(8,128)S(1)}, u32[]{:S(2)}) copy-start(f32[2,1,1024,1024]{3,2,1,0:T(8,128)S(1)} %maximum_add_fusion.3) | copy-start | bytes 25165828 | tf_op jit(solution)/shard_map/while
  75.0 28.5 %all-gather.10.cloned.1.call-start = ((), (), s32[]{:S(2)}) async-start(), calls=%async_computation.1 | async-start | bytes 2621440 | tf_op jit(solution)/shard_map/while/body/eval_jaxpr/all_gather | solution.py:15
  79.9 11.3 %collective-permute-start = (bf16[2,1,128,1024]{3,2,1,0:T(8,128)(2,1)S(1)}, bf16[2,1,128,1024]{3,2,1,0:T(8,128)(2,1)S(1)}, u32[]{:S(2)}, u32[]{:S(2)}) collective-permute-start(bf16[2,1,128,1024]{3,2,1,0:T(8,128)(2,1)S(1)} %dynamic-slice_select_fusion.6), channel_id=1, source_target_pairs={{0,1},{1,0},{2,3},{3,2},{4,5},{5,4},{6,7},{7,6},{8,9},{9,8},{10,11... | collective-permute-start | bytes 1572872 | tf_op jit(solution)/shard_map/while/body/eval_jaxpr/ppermute | solution.py:27
  83.1 11.0 %slice-start = ((s8[8388608]{0:T(1024)(128)(4,1)}), s8[4194304]{0:T(1024)(128)(4,1)S(1)}, s32[]{:S(2)}) async-start(s8[8388608]{0:T(1024)(128)(4,1)} %bitcast.97), calls=%async_computation.2 | async-start | bytes 8388608 | tf_op jit(solution)/shard_map/while
  83.8 10.3 %slice-start.1 = ((s8[8388608]{0:T(1024)(128)(4,1)}), s8[4194304]{0:T(1024)(128)(4,1)S(1)}, s32[]{:S(2)}) async-start(s8[8388608]{0:T(1024)(128)(4,1)} %bitcast.97), calls=%async_computation.3 | async-start | bytes 8388608 | tf_op jit(solution)/shard_map/while
  92.5 10.7 %collective-permute-start.1 = (bf16[2,1,128,1024]{3,2,1,0:T(8,128)(2,1)S(1)}, bf16[2,1,128,1024]{3,2,1,0:T(8,128)(2,1)S(1)}, u32[]{:S(2)}, u32[]{:S(2)}) collective-permute-start(bf16[2,1,128,1024]{3,2,1,0:T(8,128)(2,1)S(1)} %fusion.62), channel_id=1, source_target_pairs={{0,2},{2,0},{1,3},{3,1},{4,6},{6,4},{5,7},{7,5},{8,10},{10,8},{9,1... | collective-permute-start | bytes 1572872 | tf_op jit(solution)/shard_map/while/body/eval_jaxpr/ppermute | solution.py:27
  96.6 3.2 %copy-start.2 = (f32[2,1,1024,1024]{3,2,1,0:T(8,128)}, f32[2,1,1024,1024]{3,2,1,0:T(8,128)S(1)}, u32[]{:S(2)}) copy-start(f32[2,1,1024,1024]{3,2,1,0:T(8,128)S(1)} %maximum_add_fusion.3) | copy-start | bytes 25165828 | tf_op jit(solution)/shard_map/while
  105.4 31.2 %all-gather.10.cloned.1.call-start = ((), (), s32[]{:S(2)}) async-start(), calls=%async_computation.1 | async-start | bytes 2621440 | tf_op jit(solution)/shard_map/while/body/eval_jaxpr/all_gather | solution.py:15
  110.3 12.8 %collective-permute-start = (bf16[2,1,128,1024]{3,2,1,0:T(8,128)(2,1)S(1)}, bf16[2,1,128,1024]{3,2,1,0:T(8,128)(2,1)S(1)}, u32[]{:S(2)}, u32[]{:S(2)}) collective-permute-start(bf16[2,1,128,1024]{3,2,1,0:T(8,128)(2,1)S(1)} %dynamic-slice_select_fusion.6), channel_id=1, source_target_pairs={{0,1},{1,0},{2,3},{3,2},{4,5},{5,4},{6,7},{7,6},{8,9},{9,8},{10,11... | collective-permute-start | bytes 1572872 | tf_op jit(solution)/shard_map/while/body/eval_jaxpr/ppermute | solution.py:27
  114.3 11.7 %slice-start = ((s8[8388608]{0:T(1024)(128)(4,1)}), s8[4194304]{0:T(1024)(128)(4,1)S(1)}, s32[]{:S(2)}) async-start(s8[8388608]{0:T(1024)(128)(4,1)} %bitcast.97), calls=%async_computation.2 | async-start | bytes 8388608 | tf_op jit(solution)/shard_map/while
  115.0 11.0 %slice-start.1 = ((s8[8388608]{0:T(1024)(128)(4,1)}), s8[4194304]{0:T(1024)(128)(4,1)S(1)}, s32[]{:S(2)}) async-start(s8[8388608]{0:T(1024)(128)(4,1)} %bitcast.97), calls=%async_computation.3 | async-start | bytes 8388608 | tf_op jit(solution)/shard_map/while
  124.4 12.0 %collective-permute-start.1 = (bf16[2,1,128,1024]{3,2,1,0:T(8,128)(2,1)S(1)}, bf16[2,1,128,1024]{3,2,1,0:T(8,128)(2,1)S(1)}, u32[]{:S(2)}, u32[]{:S(2)}) collective-permute-start(bf16[2,1,128,1024]{3,2,1,0:T(8,128)(2,1)S(1)} %fusion.62), channel_id=1, source_target_pairs={{0,2},{2,0},{1,3},{3,1},{4,6},{6,4},{5,7},{7,5},{8,10},{10,8},{9,1... | collective-permute-start | bytes 1572872 | tf_op jit(solution)/shard_map/while/body/eval_jaxpr/ppermute | solution.py:27
  128.5 3.2 %copy-start.2 = (f32[2,1,1024,1024]{3,2,1,0:T(8,128)}, f32[2,1,1024,1024]{3,2,1,0:T(8,128)S(1)}, u32[]{:S(2)}) copy-start(f32[2,1,1024,1024]{3,2,1,0:T(8,128)S(1)} %maximum_add_fusion.3) | copy-start | bytes 25165828 | tf_op jit(solution)/shard_map/while
  140.0 3.6 %slice-start.2 = ((s8[8388608]{0:T(1024)(128)(4,1)}), s8[4194304]{0:T(1024)(128)(4,1)S(1)}, s32[]{:S(2)}) async-start(s8[8388608]{0:T(1024)(128)(4,1)} %bitcast.99), calls=%async_computation.4 | async-start | bytes 8388608
  140.7 4.4 %slice-start.3 = ((s8[8388608]{0:T(1024)(128)(4,1)}), s8[4194304]{0:T(1024)(128)(4,1)S(1)}, s32[]{:S(2)}) async-start(s8[8388608]{0:T(1024)(128)(4,1)} %bitcast.99), calls=%async_computation.5 | async-start | bytes 8388608
  151.7 2.4 %copy-start.1 = (f32[2,2]{1,0:T(2,128)S(1)}, f32[2,2]{1,0:T(2,128)}, u32[]{:S(2)}) copy-start(f32[2,2]{1,0:T(2,128)} %param.9) | copy-start | bytes 52
Sparse Core Ops, SparseCore 0:
  9.7 25.2 all-gather.7
  46.5 23.7 all-gather.9
  78.8 23.3 all-gather.9
  109.2 22.6 all-gather.9
